TPU v7x, 768 devices: a whole 4x8x12 slice. The times are simulated.
768 devices in a mesh: ctx: 24 (over z, core), tp: 32 (over x, y).
Axes of the slice: x: 4, y: 8, z: 12, core: 2. Of those that a mesh axis runs over, the one named last changes fastest.
Arguments:
- queries: bfloat16 [12288, 4096], P('ctx', 'tp'), may hold values from -15 to 15
- keys: bfloat16 [12288, 4096], P('ctx', 'tp'), may hold values from -15 to 15, as said below
- values: bfloat16 [12288, 4096], P('ctx', 'tp'), may hold values from -6 to 6, as said below
- doc_blocks: int32 [96], replicated, may hold values from 0 to 5, never falling along the last dimension, each value on 1 to 48 neighbouring positions
Outputs:
- attended: bfloat16 [12288, 4096], P('ctx', 'tp')
Inputs may be any that keep to these rules, and one draw needn't show every extreme that they name: `doc_blocks`: ids never fall along the row; each document covers 1 to 48 blocks and one covers exactly that many. `keys`: copies of the same key-value head are equal. `values`: copies of the same key-value head are equal.
All inputs are finite; a program needn't handle non-finite values.
Results may differ from a plain program's by a relative error of at most 0.0047.
Values may be sent and summed in bfloat16 or wider, within the bound.
A program may use at most 32 MiB of HBM per device.

v0:
```python
import jax
import jax.numpy as jnp
from jax import lax
from jax.sharding import PartitionSpec as P

HD = 128
BLK = 128


def positions(rows, span_rows, shards):
    stored_block = rows // span_rows
    half_index = stored_block // 2
    span = jnp.where(stored_block % 2 == 0, half_index, 2 * shards - 1 - half_index)
    return span * span_rows + rows % span_rows


def block_scores(query_block, key_part, query_pos, query_doc, key_pos, key_doc):
    scores = jnp.einsum(
        "qgrd,kgd->grqk", query_block, key_part, preferred_element_type=jnp.float32
    ) * HD ** (-0.5)
    allowed = (query_doc[:, None] == key_doc[None, :]) & (key_pos[None, :] <= query_pos[:, None])
    return (jnp.where(allowed, scores, -1e30), allowed)


def body(queries, keys, values, doc_blocks):
    span_rows = queries.shape[0] // 2
    shards = lax.axis_size("ctx")
    shard = lax.axis_index("ctx")
    heads_here = queries.shape[1] // HD
    kv_heads = keys.shape[1] // HD
    repeat_count = heads_here // kv_heads
    query_block = min(span_rows, 128)
    block_count = 2 * span_rows // query_block
    local_rows = shard * 2 * span_rows + jnp.arange(2 * span_rows, dtype=jnp.int32)
    query_pos = positions(local_rows, span_rows, shards)
    query_doc = doc_blocks[query_pos // BLK]
    query_blocks = queries.reshape(block_count, query_block, kv_heads, repeat_count, HD)
    pos_blocks = query_pos.reshape(block_count, query_block)
    doc_query_blocks = query_doc.reshape(block_count, query_block)
    whole_keys, whole_values = (
        lax.all_gather(keys, "ctx", axis=0, tiled=True),
        lax.all_gather(values, "ctx", axis=0, tiled=True),
    )
    piece_key_pos = positions(jnp.arange(whole_keys.shape[0], dtype=jnp.int32), span_rows, shards)
    key_doc = doc_blocks[piece_key_pos // BLK]
    key_part = whole_keys.reshape(-1, kv_heads, HD)
    value_part = whole_values.reshape(-1, kv_heads, HD)

    def one_block(item):
        block, block_pos, block_doc = item
        scores, allowed = block_scores(
            block, key_part, block_pos, block_doc, piece_key_pos, key_doc
        )
        peak_value = jnp.max(scores, axis=-1, keepdims=True)
        weight = jnp.where(allowed, jnp.exp(scores - peak_value), 0.0)
        total = jnp.sum(weight, axis=-1, keepdims=True)
        probs = (weight / total).astype(jnp.bfloat16)
        return jnp.einsum("grqk,kgd->qgrd", probs, value_part, preferred_element_type=jnp.float32)

    mixed = lax.map(one_block, (query_blocks, pos_blocks, doc_query_blocks))
    return mixed.reshape(2 * span_rows, heads_here * HD).astype(jnp.bfloat16)


def solution(mesh):
    return jax.shard_map(
        body,
        mesh=mesh,
        in_specs=(P("ctx", "tp"), P("ctx", "tp"), P("ctx", "tp"), P()),
        out_specs=P("ctx", "tp"),
        check_vma=False,
    )
```

profile of v0, /device:TPU:1, one launch (start us, length us, event | category | flops | bytes accessed | tf_op | source)
XLA Modules:
  0.0 180.6 jit_solution(6166182935599261009)
XLA Ops:
  6.5 0.0 copy-start
  6.5 0.0 all-gather.3.cloned.1.call-start
  6.5 0.7 all-gather.3.cloned.1.call-update
  7.3 0.0 all-gather.5.cloned.1.call-start
  7.3 0.7 all-gather.5.cloned.1.call-update
  8.0 0.1 compare_select_fusion.8
  8.1 0.0 copy-done
  8.1 3.3 %gather_fusion = s32[512]{0:T(512)S(1)} fusion(s32[96]{0:T(128)S(1)} %copy-done, s32[1024]{0:T(1024)S(1)} %pad_clamp_fusion), kind=kCustom, calls=%fused_computation | custom fusion | bytes 6144 | tf_op jit(solution)/shard_map/gather | solution.py:36
  11.5 0.3 compare_select_fusion
  11.8 73.0 %gather_fusion.1 = s32[12288]{0:T(1024)S(1)} fusion(s32[96]{0:T(128)S(1)} %copy-done, s32[12288]{0:T(1024)S(1)} %broadcast_clamp_fusion), kind=kCustom, calls=%fused_computation.1 | custom fusion | bytes 147456 | tf_op jit(solution)/shard_map/gather | solution.py:45
  84.9 0.0 all-gather.3.cloned.1.call-done
  84.9 54.7 %all-gather.5.cloned.1.call-done = bf16[12288,128]{1,0:T(8,128)(2,1)} async-done(((bf16[512,128]{1,0:T(8,128)(2,1)}), bf16[12288,128]{1,0:T(8,128)(2,1)}) %all-gather.5.cloned.1.call-update) | async-done | bytes 3145744 | tf_op jit(solution)/shard_map/all_gather | solution.py:42
  139.6 33.5 %while.11 = (s32[]{:T(128)}, bf16[4,128,1,1,128]{4,1,3,2,0:T(8,128)(2,1)S(1)}, s32[4,128]{1,0:T(4,128)S(1)}, s32[12288]{0:T(1024)S(1)}, s32[4,128]{1,0:T(4,128)S...) while((s32[]{:T(128)}, ...), condition=%wide.region_3.4_spmd.clone, body=%wide.region_0.3_spmd.clone.sunk | while | flops 835632896 | bytes 38199424 | solution.py:60
  139.7 0.0 copy-start.1
  139.7 4.1 %fusion.61 = (f32[128]{0:T(128)S(1)}, f32[1,1,128,12288]{3,2,1,0:T(8,128)S(1)}) fusion(bf16[12288,1,128]{2,0,1:T(8,128)(2,1)} %get-tuple-element.180, bf16[4,128,1,1,128]{4,1,3,2,0:T(8,128)(2,1)} %get-tuple-element.179, s32[]{:T(128)} %get-tuple-element.165, s32[128]{0:T(128)S(1)} %get-tuple-element.152, s32[12288]{0:T(1024)S(1)} %fusion.60, ...), kind=kOutput, calls=%fused_computation.106.clone.1 | convolution fusion | flops 412090240 | bytes 9570304 | tf_op jit(solution)/shard_map/while/body/eval_jaxpr/qgrd,kgd->grqk/dot_general | solution.py:18
  143.8 1.8 %fusion.62 = f32[128]{0:T(128)S(1)} fusion(f32[1,1,128,12288]{3,2,1,0:T(8,128)S(1)} %get-tuple-element.154, f32[128]{0:T(128)S(1)} %get-tuple-element.155, s32[12288]{0:T(1024)S(1)} %fusion.60, s32[12288]{0:T(1024)S(1)} %get-tuple-element.177, s32[128]{0:T(128)S(1)} %get-tuple-element.152, s32[128]{0:T(128)S(1)} %get-tuple-element.153), kind=kLoop, calls=%fused_computation.9.clone.1 | loop fusion | flops 9437056 | bytes 6391808 | tf_op jit(solution)/shard_map/while/body/eval_jaxpr/reduce_sum | solution.py:56
  145.6 0.0 copy-done.1
  145.6 2.4 %fusion.63 = bf16[4,128,1,1,128]{4,1,3,2,0:T(8,128)(2,1)S(1)} fusion(bf16[4,128,1,1,128]{4,1,3,2,0:T(8,128)(2,1)S(1)} %get-tuple-element.166, s32[]{:T(128)} %get-tuple-element.165, bf16[12288,1,128]{2,0,1:T(8,128)(2,1)S(1)} %copy-done.1, f32[128]{0:T(128)S(1)} %fusion.62, f32[1,1,128,12288]{3,2,1,0:T(8,128)S(1)} %get-tuple-element.154, ...), kind=kOutput, calls=%fused_computation.15.clone.1 | convolution fusion | flops 413663232 | bytes 9603076 | tf_op jit(solution)/shard_map/while/body/eval_jaxpr/grqk,kgd->qgrd/dot_general | solution.py:58
  148.0 0.0 copy-start.1
  148.0 4.1 %fusion.61 = (f32[128]{0:T(128)S(1)}, f32[1,1,128,12288]{3,2,1,0:T(8,128)S(1)}) fusion(bf16[12288,1,128]{2,0,1:T(8,128)(2,1)} %get-tuple-element.180, bf16[4,128,1,1,128]{4,1,3,2,0:T(8,128)(2,1)} %get-tuple-element.179, s32[]{:T(128)} %get-tuple-element.165, s32[128]{0:T(128)S(1)} %get-tuple-element.152, s32[12288]{0:T(1024)S(1)} %fusion.60, ...), kind=kOutput, calls=%fused_computation.106.clone.1 | convolution fusion | flops 412090240 | bytes 9570304 | tf_op jit(solution)/shard_map/while/body/eval_jaxpr/qgrd,kgd->grqk/dot_general | solution.py:18
  152.1 1.8 %fusion.62 = f32[128]{0:T(128)S(1)} fusion(f32[1,1,128,12288]{3,2,1,0:T(8,128)S(1)} %get-tuple-element.154, f32[128]{0:T(128)S(1)} %get-tuple-element.155, s32[12288]{0:T(1024)S(1)} %fusion.60, s32[12288]{0:T(1024)S(1)} %get-tuple-element.177, s32[128]{0:T(128)S(1)} %get-tuple-element.152, s32[128]{0:T(128)S(1)} %get-tuple-element.153), kind=kLoop, calls=%fused_computation.9.clone.1 | loop fusion | flops 9437056 | bytes 6391808 | tf_op jit(solution)/shard_map/while/body/eval_jaxpr/reduce_sum | solution.py:56
  154.0 0.0 copy-done.1
  154.0 2.4 %fusion.63 = bf16[4,128,1,1,128]{4,1,3,2,0:T(8,128)(2,1)S(1)} fusion(bf16[4,128,1,1,128]{4,1,3,2,0:T(8,128)(2,1)S(1)} %get-tuple-element.166, s32[]{:T(128)} %get-tuple-element.165, bf16[12288,1,128]{2,0,1:T(8,128)(2,1)S(1)} %copy-done.1, f32[128]{0:T(128)S(1)} %fusion.62, f32[1,1,128,12288]{3,2,1,0:T(8,128)S(1)} %get-tuple-element.154, ...), kind=kOutput, calls=%fused_computation.15.clone.1 | convolution fusion | flops 413663232 | bytes 9603076 | tf_op jit(solution)/shard_map/while/body/eval_jaxpr/grqk,kgd->qgrd/dot_general | solution.py:58
  156.4 4.1 %fusion.61 = (f32[128]{0:T(128)S(1)}, f32[1,1,128,12288]{3,2,1,0:T(8,128)S(1)}) fusion(bf16[12288,1,128]{2,0,1:T(8,128)(2,1)} %get-tuple-element.180, bf16[4,128,1,1,128]{4,1,3,2,0:T(8,128)(2,1)} %get-tuple-element.179, s32[]{:T(128)} %get-tuple-element.165, s32[128]{0:T(128)S(1)} %get-tuple-element.152, s32[12288]{0:T(1024)S(1)} %fusion.60, ...), kind=kOutput, calls=%fused_computation.106.clone.1 | convolution fusion | flops 412090240 | bytes 9570304 | tf_op jit(solution)/shard_map/while/body/eval_jaxpr/qgrd,kgd->grqk/dot_general | solution.py:18
  160.5 1.8 %fusion.62 = f32[128]{0:T(128)S(1)} fusion(f32[1,1,128,12288]{3,2,1,0:T(8,128)S(1)} %get-tuple-element.154, f32[128]{0:T(128)S(1)} %get-tuple-element.155, s32[12288]{0:T(1024)S(1)} %fusion.60, s32[12288]{0:T(1024)S(1)} %get-tuple-element.177, s32[128]{0:T(128)S(1)} %get-tuple-element.152, s32[128]{0:T(128)S(1)} %get-tuple-element.153), kind=kLoop, calls=%fused_computation.9.clone.1 | loop fusion | flops 9437056 | bytes 6391808 | tf_op jit(solution)/shard_map/while/body/eval_jaxpr/reduce_sum | solution.py:56
  162.4 2.4 %fusion.63 = bf16[4,128,1,1,128]{4,1,3,2,0:T(8,128)(2,1)S(1)} fusion(bf16[4,128,1,1,128]{4,1,3,2,0:T(8,128)(2,1)S(1)} %get-tuple-element.166, s32[]{:T(128)} %get-tuple-element.165, bf16[12288,1,128]{2,0,1:T(8,128)(2,1)S(1)} %copy-done.1, f32[128]{0:T(128)S(1)} %fusion.62, f32[1,1,128,12288]{3,2,1,0:T(8,128)S(1)} %get-tuple-element.154, ...), kind=kOutput, calls=%fused_computation.15.clone.1 | convolution fusion | flops 413663232 | bytes 9603076 | tf_op jit(solution)/shard_map/while/body/eval_jaxpr/grqk,kgd->qgrd/dot_general | solution.py:58
  164.8 4.1 %fusion.61 = (f32[128]{0:T(128)S(1)}, f32[1,1,128,12288]{3,2,1,0:T(8,128)S(1)}) fusion(bf16[12288,1,128]{2,0,1:T(8,128)(2,1)} %get-tuple-element.180, bf16[4,128,1,1,128]{4,1,3,2,0:T(8,128)(2,1)} %get-tuple-element.179, s32[]{:T(128)} %get-tuple-element.165, s32[128]{0:T(128)S(1)} %get-tuple-element.152, s32[12288]{0:T(1024)S(1)} %fusion.60, ...), kind=kOutput, calls=%fused_computation.106.clone.1 | convolution fusion | flops 412090240 | bytes 9570304 | tf_op jit(solution)/shard_map/while/body/eval_jaxpr/qgrd,kgd->grqk/dot_general | solution.py:18
  168.9 1.8 %fusion.62 = f32[128]{0:T(128)S(1)} fusion(f32[1,1,128,12288]{3,2,1,0:T(8,128)S(1)} %get-tuple-element.154, f32[128]{0:T(128)S(1)} %get-tuple-element.155, s32[12288]{0:T(1024)S(1)} %fusion.60, s32[12288]{0:T(1024)S(1)} %get-tuple-element.177, s32[128]{0:T(128)S(1)} %get-tuple-element.152, s32[128]{0:T(128)S(1)} %get-tuple-element.153), kind=kLoop, calls=%fused_computation.9.clone.1 | loop fusion | flops 9437056 | bytes 6391808 | tf_op jit(solution)/shard_map/while/body/eval_jaxpr/reduce_sum | solution.py:56
  170.7 0.0 copy-done.1
  170.7 2.4 %fusion.63 = bf16[4,128,1,1,128]{4,1,3,2,0:T(8,128)(2,1)S(1)} fusion(bf16[4,128,1,1,128]{4,1,3,2,0:T(8,128)(2,1)S(1)} %get-tuple-element.166, s32[]{:T(128)} %get-tuple-element.165, bf16[12288,1,128]{2,0,1:T(8,128)(2,1)S(1)} %copy-done.1, f32[128]{0:T(128)S(1)} %fusion.62, f32[1,1,128,12288]{3,2,1,0:T(8,128)S(1)} %get-tuple-element.154, ...), kind=kOutput, calls=%fused_computation.15.clone.1 | convolution fusion | flops 413663232 | bytes 9603076 | tf_op jit(solution)/shard_map/while/body/eval_jaxpr/grqk,kgd->qgrd/dot_general | solution.py:58
  173.1 0.0 copy-start.2
  173.1 0.6 copy-done.2
  (15 shorter events, 0.2 us)
Async XLA Ops:
  6.5 1.6 copy-start
  6.5 78.4 %all-gather.3.cloned.1.call-start = ((), (), s32[]{:S(2)}) async-start(), calls=%async_computation | async-start | bytes 3276800 | tf_op jit(solution)/shard_map/all_gather | solution.py:41
  7.3 132.4 %all-gather.5.cloned.1.call-start = ((), (), s32[]{:S(2)}) async-start(), calls=%async_computation.1 | async-start | bytes 3276800 | tf_op jit(solution)/shard_map/all_gather | solution.py:42
  139.7 6.0 %copy-start.1 = (bf16[12288,1,128]{2,0,1:T(8,128)(2,1)S(1)}, bf16[12288,1,128]{2,0,1:T(8,128)(2,1)}, u32[]{:S(2)}) copy-start(bf16[12288,1,128]{2,0,1:T(8,128)(2,1)} %get-tuple-element.181) | copy-start | bytes 9437188 | tf_op jit(solution)/shard_map/while
  148.0 6.0 %copy-start.1 = (bf16[12288,1,128]{2,0,1:T(8,128)(2,1)S(1)}, bf16[12288,1,128]{2,0,1:T(8,128)(2,1)}, u32[]{:S(2)}) copy-start(bf16[12288,1,128]{2,0,1:T(8,128)(2,1)} %get-tuple-element.181) | copy-start | bytes 9437188 | tf_op jit(solution)/shard_map/while
  156.4 6.0 %copy-start.1 = (bf16[12288,1,128]{2,0,1:T(8,128)(2,1)S(1)}, bf16[12288,1,128]{2,0,1:T(8,128)(2,1)}, u32[]{:S(2)}) copy-start(bf16[12288,1,128]{2,0,1:T(8,128)(2,1)} %get-tuple-element.181) | copy-start | bytes 9437188 | tf_op jit(solution)/shard_map/while
  164.8 6.0 %copy-start.1 = (bf16[12288,1,128]{2,0,1:T(8,128)(2,1)S(1)}, bf16[12288,1,128]{2,0,1:T(8,128)(2,1)}, u32[]{:S(2)}) copy-start(bf16[12288,1,128]{2,0,1:T(8,128)(2,1)} %get-tuple-element.181) | copy-start | bytes 9437188 | tf_op jit(solution)/shard_map/while
  173.1 0.7 copy-start.2
Sparse Core Ops, SparseCore 0:
  9.8 69.1 all-gather.2
  81.5 58.1 all-gather.4
where the time goes:
time: 181 us
  local copies, waits for them, and re-layouts  77.1 us (43%)
  waiting for transfers between devices  56.1 us (31%)
  matrix products  25.8 us (14%)
  between operations  13.5 us (7%)
  other arithmetic  7.94 us (4%)
    gather x1, local copies, waits for them, and re-layouts, body(): key_doc = doc_blocks[piece_key_pos // BLK]  73 us
    all_gather x1, waiting for transfers between devices, body(): lax.all_gather(values, 'ctx', axis=0, tiled=True)  54.7 us
    dot_general x4, matrix products, block_scores(): jnp.einsum('qgrd,kgd->grqk', query_block, key_part, preferred_element_typ...  16.4 us
    dot_general x4, matrix products, one_block(): jnp.einsum('grqk,kgd->qgrd', probs, value_part, preferred_element_type=jn...  9.41 us
    reduce_sum x4, other arithmetic, one_block(): total = jnp.sum(weight, axis=-1, keepdims=True)  7.39 us
  transfers between devices with their start and end apart: 2, of which 1 were waited for; matrix products, arithmetic and copies ran while one was open for 43% of the time, Pallas kernels for 0%

commit v1 on v0

v1 whole, which is shorter than its diff:
```python
import functools

import jax
import jax.numpy as jnp
from jax import lax
from jax.experimental import pallas as pl
from jax.experimental.pallas import tpu as pltpu
from jax.sharding import PartitionSpec as P

HD = 128
BLK = 128
SPAN = 256
SHARE = 80
RING = SPAN - SHARE
MESH = pl.DeviceIdType.MESH
LOG2E = 1.4426950408889634
SCALE = HD**-0.5 * LOG2E
NEG = -1e30


def kernel(
    chips,
    doc_ref, q_hbm, k_hbm, v_hbm, out_ref,
    q_ref, kv, acc, peak, total,
    load_sem, ring_send, ring_recv, side_send, side_recv,
    mate_send, mate_recv, mate_side_send, mate_side_recv,
):
    ctx, tp = lax.axis_index("ctx"), lax.axis_index("tp")
    z, core = ctx // 2, ctx % 2
    odd = tp % 2
    shards = 2 * chips
    up = (lax.rem(ctx + 2, shards), tp)
    down = (lax.rem(ctx + shards - 2, shards), tp)
    mate = (2 * z + 1 - core, tp)
    side = (ctx, tp + 1 - 2 * odd)
    other = 1 - core

    loads = []
    for kind in range(2):
        for part, hbm in enumerate((k_hbm, v_hbm)):
            loads.append(
                pltpu.make_async_copy(
                    hbm.at[pl.ds(kind * SPAN, SPAN)], kv.at[z, kind, part, core], load_sem.at[2 * kind + part]
                )
            )
    loads.append(pltpu.make_async_copy(q_hbm, q_ref, load_sem.at[4]))
    for copy in loads:
        copy.start()

    barrier = pltpu.get_barrier_semaphore()
    for neighbour in (up, down, mate, side):
        pl.semaphore_signal(barrier, inc=1, device_id=neighbour, device_id_type=MESH)
    pl.semaphore_wait(barrier, 4)

    ring_at = pl.multiple_of(odd * SHARE, 16)
    give_at = pl.multiple_of(odd * RING, 16)
    take_at = pl.multiple_of((1 - odd) * RING, 16)

    def remote(ref, sends, recvs, index, device):
        return pltpu.make_async_remote_copy(
            src_ref=ref,
            dst_ref=ref,
            send_sem=sends.at[index],
            recv_sem=recvs.at[index],
            device_id=device,
            device_id_type=MESH,
        )

    def ring_copy(s, kind, device):
        return remote(
            kv.at[s, kind, :, core, pl.ds(ring_at, RING)], ring_send, ring_recv, (s, kind), device
        )

    def ring_arrival(s, kind):
        return ring_copy(s, kind, up)

    def side_copy(s, kind):
        return remote(kv.at[s, kind, :, core, pl.ds(give_at, SHARE)], side_send, side_recv, (s, kind), side)

    def side_arrival(s, kind):
        return remote(kv.at[s, kind, :, core, pl.ds(take_at, SHARE)], side_send, side_recv, (s, kind), side)

    def mate_ring(s, kind, who):
        return remote(kv.at[s, kind, :, who, pl.ds(ring_at, RING)], mate_send, mate_recv, (s, kind), mate)

    def mate_side(s, kind, who):
        return remote(
            kv.at[s, kind, :, who, pl.ds(take_at, SHARE)], mate_side_send, mate_side_recv, (s, kind), mate
        )

    def mate_own(kind, who):
        return remote(kv.at[z, kind, :, who], mate_send, mate_recv, (z, kind), mate)

    def own_second(kind, device, sems):
        return remote(
            kv.at[z, kind, :, core, pl.ds(ring_at, RING)], sems, ring_recv, (z, kind), device
        )

    for kind in range(2):
        loads[2 * kind].wait()
        loads[2 * kind + 1].wait()
        own_second(kind, up, ring_send).start()
        own_second(kind, down, side_send).start()
        mate_own(kind, core).start()
    loads[4].wait()

    low_block = 2 * ctx
    high_block = 2 * (2 * shards - 1 - ctx)

    def first_block(s, kind, j):
        return 2 * (2 * s + j) if kind == 0 else 2 * (2 * shards - 1 - 2 * s - j)

    def own(row, q_block, kind):
        q = q_ref[pl.ds(row, BLK)]
        k = kv[z, kind, 0].reshape(2 * SPAN, HD)
        v = kv[z, kind, 1].reshape(2 * SPAN, HD)
        s = lax.dot_general(q, k, (((1,), (1,)), ((), ())), preferred_element_type=jnp.float32)
        inside = lax.broadcasted_iota(jnp.int32, (BLK, BLK), 1) <= lax.broadcasted_iota(jnp.int32, (BLK, BLK), 0)
        parts = []
        for j in range(2):
            for half in range(2):
                k_block = first_block(z, kind, j) + half
                at = (2 * j + half) * BLK
                same = doc_ref[k_block] == doc_ref[q_block]
                before = jnp.where(same & (k_block < q_block), 0.0, NEG)
                at_or_before = jnp.where(same & (k_block <= q_block), 0.0, NEG)
                parts.append(s[:, at : at + BLK] * SCALE + jnp.where(inside, at_or_before, before))
        most = functools.reduce(jnp.maximum, parts)
        top = jnp.broadcast_to(jnp.max(most, axis=1, keepdims=True), (BLK, HD))
        weights = [jnp.exp2(part - top) for part in parts]
        peak[pl.ds(row, BLK)] = top
        total[pl.ds(row, BLK)] = functools.reduce(jnp.add, weights)
        joined = jnp.concatenate([w.astype(jnp.bfloat16) for w in weights], axis=1)
        acc[pl.ds(row, BLK)] = jnp.dot(joined, v, preferred_element_type=jnp.float32)

    def unit(row, q_block, s_chip, kind):
        q = q_ref[pl.ds(row, BLK)]
        k = kv[s_chip, kind, 0].reshape(2 * SPAN, HD)
        v = kv[s_chip, kind, 1].reshape(2 * SPAN, HD)
        s = lax.dot_general(q, k, (((1,), (1,)), ((), ())), preferred_element_type=jnp.float32)
        parts = []
        for j in range(2):
            for half in range(2):
                k_block = first_block(s_chip, kind, j) + half
                at = (2 * j + half) * BLK
                bias = jnp.where(doc_ref[k_block] == doc_ref[q_block], 0.0, NEG)
                parts.append(s[:, at : at + BLK] * SCALE + bias)
        most = functools.reduce(jnp.maximum, parts)
        old = peak[pl.ds(row, BLK)]
        top = jnp.maximum(old, jnp.max(most, axis=1, keepdims=True))
        shrink = jnp.exp2(old - top)
        weights = [jnp.exp2(part - top) for part in parts]
        peak[pl.ds(row, BLK)] = top
        total[pl.ds(row, BLK)] = total[pl.ds(row, BLK)] * shrink + functools.reduce(jnp.add, weights)
        joined = jnp.concatenate([w.astype(jnp.bfloat16) for w in weights], axis=1)
        acc[pl.ds(row, BLK)] = acc[pl.ds(row, BLK)] * shrink + jnp.dot(
            joined, v, preferred_element_type=jnp.float32
        )

    def units(base, q_first, s_chip, kind):
        for half in range(2):
            unit(base + half * BLK, q_first + half, s_chip, kind)

    for kind in range(2):
        mate_own(kind, other).wait_recv()
    for half in range(2):
        own(half * BLK, low_block + half, 0)
        own(SPAN + half * BLK, high_block + half, 1)

    @pl.when(z + z >= chips - 1)
    def _():
        units(SPAN, high_block, z, 0)

    def source(way, h):
        return lax.rem(z + 2 * chips - h, chips) if way == 0 else lax.rem(z + h, chips)

    half_ring = chips // 2
    limit = {(0, 0): half_ring, (1, 0): half_ring - 1, (0, 1): half_ring - 1, (1, 1): half_ring}

    def step(h, carry):
        for kind in range(2):
            for way in range(2):

                @pl.when(h <= limit[way, kind])
                def _():
                    s = source(way, h)
                    ring_arrival(s, kind).wait_recv()

                    @pl.when(h < limit[way, kind])
                    def _():
                        ring_copy(s, kind, up if way == 0 else down).start()

                    side_copy(s, kind).start()
                    mate_ring(s, kind, core).start()

        for kind in range(2):
            for way in range(2):

                @pl.when((h >= 2) & (h - 1 <= limit[way, kind]))
                def _():
                    s = source(way, h - 1)
                    side_arrival(s, kind).wait_recv()
                    mate_side(s, kind, core).start()

        for kind in range(2):
            for way in range(2):

                @pl.when((h >= 3) & (h - 2 <= limit[way, kind]))
                def _():
                    s = source(way, h - 2)
                    mate_ring(s, kind, other).wait_recv()
                    mate_side(s, kind, other).wait_recv()
                    if kind == 0:

                        @pl.when(s < z)
                        def _():
                            units(0, low_block, s, 0)

                        @pl.when(s + z >= chips - 1)
                        def _():
                            units(SPAN, high_block, s, 0)
                    else:

                        @pl.when(s > z)
                        def _():
                            units(SPAN, high_block, s, 1)

        return carry

    lax.fori_loop(1, half_ring + 3, step, 0)

    for row in range(0, 2 * SPAN, BLK):
        rows = pl.ds(row, BLK)
        out_ref[rows] = (acc[rows] / jnp.sum(total[rows], axis=1, keepdims=True)).astype(out_ref.dtype)

    for kind in range(2):
        own_second(kind, up, ring_send).wait_send()
        own_second(kind, down, side_send).wait_send()
        mate_own(kind, core).wait_send()

    def drain(h, carry):
        for kind in range(2):
            for way in range(2):

                @pl.when(h <= limit[way, kind])
                def _():
                    s = source(way, h)

                    @pl.when(h < limit[way, kind])
                    def _():
                        ring_copy(s, kind, up).wait_send()

                    side_copy(s, kind).wait_send()
                    mate_ring(s, kind, core).wait_send()
                    mate_side(s, kind, core).wait_send()

        return carry

    lax.fori_loop(1, half_ring + 1, drain, 0)


def body(queries, keys, values, doc_blocks):
    rows = queries.shape[0]
    chips = lax.axis_size("ctx") // 2
    sems = pltpu.SemaphoreType.DMA((chips, 2))
    return pl.pallas_call(
        functools.partial(kernel, chips),
        out_shape=jax.ShapeDtypeStruct((rows, HD), jnp.bfloat16),
        in_specs=[pl.BlockSpec(memory_space=pltpu.SMEM)] + [pl.BlockSpec(memory_space=pl.ANY)] * 3,
        out_specs=pl.BlockSpec(memory_space=pltpu.VMEM),
        scratch_shapes=[
            pltpu.VMEM((rows, HD), jnp.bfloat16),
            pltpu.VMEM((chips, 2, 2, 2, SPAN, HD), jnp.bfloat16),
            pltpu.VMEM((rows, HD), jnp.float32),
            pltpu.VMEM((rows, HD), jnp.float32),
            pltpu.VMEM((rows, HD), jnp.float32),
            pltpu.SemaphoreType.DMA((5,)),
        ]
        + [sems] * 8,
        compiler_params=pltpu.CompilerParams(collective_id=0, has_side_effects=True),
    )(doc_blocks, queries, keys, values)


def solution(mesh):
    return jax.shard_map(
        body,
        mesh=mesh,
        in_specs=(P("ctx", "tp"), P("ctx", "tp"), P("ctx", "tp"), P()),
        out_specs=P("ctx", "tp"),
        check_vma=False,
    )
```

time: 181 us -> 52.2 us (0.29)
  local copies, waits for them, and re-layouts: 77.1 us -> 1.57 us
  waiting for transfers between devices: 56.1 us -> 0 us
  Pallas kernels: 0 us -> 50.5 us
  matrix products: 25.8 us -> 0 us
  between operations: 13.5 us -> 0.01 us
  other arithmetic: 7.94 us -> 0 us
    gather x2 -> x0, local copies, waits for them, and re-layouts: 76.4 us -> none  [the longest x1 73 us: body(): key_doc = doc_blocks[piece_key_pos // BLK]]
    all_gather x2 -> x0, waiting for transfers between devices: 54.7 us -> none  [the longest x1 54.7 us: body(): lax.all_gather(values, 'ctx', axis=0, tiled=True)]
    pallas_call x0 -> x1, Pallas kernels: none -> 50.5 us  [body(): pl.pallas_call(functools.partial(kernel, chips), out_shape=jax.ShapeDtype...]
    dot_general x8 -> x0, matrix products: 25.8 us -> none  [the longest x4 16.4 us: block_scores(): jnp.einsum('qgrd,kgd->grqk', query_block, key_part, preferred_element_typ...]
    reduce_sum x4 -> x0, other arithmetic: 7.39 us -> none  [one_block(): total = jnp.sum(weight, axis=-1, keepdims=True)]
  transfers between devices with their start and end apart: 2 -> 0, of which waited for: 1 -> 0; matrix products, arithmetic and copies ran while one was open for 43% -> 0% of each run, Pallas kernels for 0% -> 0%
where the time goes in v1:
time: 52.2 us; the launch traced here: 52.1 us
  Pallas kernels  50.5 us (97%)
  local copies, waits for them, and re-layouts  1.57 us (3%)
    pallas_call x1, Pallas kernels, body(): pl.pallas_call(functools.partial(kernel, chips), out_shape=jax.ShapeDtype...  50.5 us
    unnamed x1, local copies, waits for them, and re-layouts  1.57 us

profile of v1, /device:TPU:1, one launch (start us, length us, event | category | flops | bytes accessed | tf_op | source)
XLA Modules:
  0.0 52.1 jit_solution(13501899995967148216)
XLA Ops:
  0.0 50.5 %shard_map.46 = bf16[512,128]{1,0:T(8,128)(2,1)} custom-call(s32[96]{0:T(128)} %doc_ref.1, bf16[512,128]{1,0:T(8,128)(2,1)} %q_hbm.1, bf16[512,128]{1,0:T(8,128)(2,1)} %k_hbm.1, bf16[512,128]{1,0:T(8,128)(2,1)} %v_hbm.1), custom_call_target="tpu_custom_call" | custom-call | tf_op jit(solution)/shard_map/pallas_call | solution.py:266
  50.5 1.6 %copy.6 = bf16[512,128]{1,0:T(8,128)(2,1)} copy(bf16[512,128]{1,0:T(8,128)(2,1)} %shard_map.46) | data formatting | bytes 262144

commit v2 on v0

v2 whole, which is shorter than its diff:
```python
import functools

import jax
import jax.numpy as jnp
from jax import lax
from jax.experimental import pallas as pl
from jax.experimental.pallas import tpu as pltpu
from jax.sharding import PartitionSpec as P

HD = 128
BLK = 128
SPAN = 256
LONGEST = 48
STARTS = 4
MESH = pl.DeviceIdType.MESH
LOG2E = 1.4426950408889634
SCALE = HD**-0.5 * LOG2E
NEG = -1e30
FLOOR = -1e29
NONE = 15

PLANS = [
    (
        [
            [-1, 0, 1, 2, 3, 7, 8, 10, 10, 11, 0, 1],
            [-1, -1, 3, 1, 3, 4, 4, 9, 9, 11, 11, 1],
            [-1, -1, -1, 2, 2, 6, 4, 6, 6, 10, 11, 3],
            [-1, -1, -1, -1, 3, 4, 4, 3, 7, 11, 11, 3],
            [-1, -1, -1, -1, -1, 6, 4, 5, 6, 7, 8, 10],
            [-1, -1, -1, -1, -1, -1, 5, 8, 6, 8, 8, 9],
            [-1, -1, -1, -1, -1, -1, -1, 6, 6, 8, 8, 9],
            [-1, -1, -1, -1, -1, -1, -1, -1, 7, 10, 8, 10],
            [-1, -1, -1, -1, -1, -1, -1, -1, -1, 8, 11, 9],
            [-1, -1, -1, -1, -1, -1, -1, -1, -1, -1, 9, 10],
            [-1, -1, -1, -1, -1, -1, -1, -1, -1, -1, -1, 10],
            [-1, -1, -1, -1, -1, -1, -1, -1, -1, -1, -1, -1],
        ],
        [
            [-1, -1, -1, -1, -1, -1, -1, -1, -1, -1, -1, -1],
            [1, -1, -1, -1, -1, -1, -1, -1, -1, -1, -1, -1],
            [2, 2, -1, -1, -1, -1, -1, -1, -1, -1, -1, -1],
            [2, 0, 3, -1, -1, -1, -1, -1, -1, -1, -1, -1],
            [1, 2, 4, 2, -1, -1, -1, -1, -1, -1, -1, -1],
            [2, 2, 3, 5, 2, -1, -1, -1, -1, -1, -1, -1],
            [2, 2, 5, 4, 5, 6, -1, -1, -1, -1, -1, -1],
            [5, 0, 5, 4, 5, 7, 7, -1, -1, -1, -1, -1],
            [8, 0, 1, 1, 0, 4, 8, 6, -1, -1, -1, -1],
            [8, 0, 5, 5, 5, 8, 5, 8, 9, -1, -1, -1],
            [10, 2, 0, 2, 6, 6, 10, 6, 9, 10, -1, -1],
            [11, 0, 1, 6, 6, 6, 8, 8, 11, 10, 11, -1],
        ],
        [
            [5, 3, 17, 21, 23, 19, 7, 15, 13, 9, 11],
            [5, 0, 9, 17, 23, 13, 19, 7, 11, 15, 21],
            [9, 7, 0, 13, 11, 15, 2, 21, 17, 19, 23],
            [4, 11, 2, 9, 13, 0, 19, 17, 15, 21, 23],
            [4, 6, 13, 2, 15, 21, 17, 19, 11, 0, 23],
            [13, 15, 8, 6, 19, 2, 21, 4, 0, 17, 23],
            [8, 10, 15, 17, 21, 4, 6, 23, 2, 0, 19],
            [12, 6, 19, 0, 17, 21, 23, 8, 4, 2, 10],
            [19, 12, 14, 23, 8, 0, 10, 21, 6, 2, 4],
            [16, 21, 12, 2, 23, 6, 10, 0, 14, 4, 8],
            [0, 18, 23, 12, 2, 14, 6, 4, 8, 16, 10],
            [2, 20, 6, 4, 0, 16, 18, 12, 14, 8, 10],
        ],
    ),
    (
        [
            [-1, 0, -1, -1, -1, -1, -1, -1, -1, -1, -1, -1],
            [-1, -1, 1, 1, 2, 4, 4, 8, 10, 10, 1, 10],
            [-1, -1, -1, 4, 2, 3, 5, 9, 9, 4, 9, 10],
            [-1, -1, -1, -1, 5, 3, 7, 5, 6, 7, 9, 10],
            [-1, -1, -1, -1, -1, 6, 4, 6, 7, 7, 9, 8],
            [-1, -1, -1, -1, -1, -1, 5, 5, 7, 10, 7, 10],
            [-1, -1, -1, -1, -1, -1, -1, 6, 9, 7, 8, 9],
            [-1, -1, -1, -1, -1, -1, -1, -1, 7, 10, 8, 10],
            [-1, -1, -1, -1, -1, -1, -1, -1, -1, 8, 8, 10],
            [-1, -1, -1, -1, -1, -1, -1, -1, -1, -1, 9, 10],
            [-1, -1, -1, -1, -1, -1, -1, -1, -1, -1, -1, 10],
            [-1, -1, -1, -1, -1, -1, -1, -1, -1, -1, 11, -1],
        ],
        [
            [-1, -1, -1, -1, -1, -1, -1, -1, -1, -1, -1, -1],
            [1, -1, -1, -1, -1, -1, -1, -1, -1, -1, -1, -1],
            [2, 2, -1, -1, -1, -1, -1, -1, -1, -1, -1, -1],
            [2, 3, 3, -1, -1, -1, -1, -1, -1, -1, -1, -1],
            [2, 2, 4, 2, -1, -1, -1, -1, -1, -1, -1, -1],
            [1, 3, 3, 5, 3, -1, -1, -1, -1, -1, -1, -1],
            [1, 6, 1, 1, 3, 6, -1, -1, -1, -1, -1, -1],
            [7, 0, 5, 2, 5, 7, 7, -1, -1, -1, -1, -1],
            [7, 8, 1, 1, 5, 6, 7, 8, -1, -1, -1, -1],
            [9, 0, 5, 5, 5, 8, 7, 8, 9, -1, -1, -1],
            [10, 0, 5, 5, 3, 10, 5, 8, 10, 10, -1, -1],
            [-1, -1, -1, -1, -1, -1, -1, -1, -1, -1, 11, -1],
        ],
        [
            [5, 3, 15, 7, 19, 13, 21, 9, 11, 17],
            [0, 5, 7, 13, 11, 17, 15, 9, 19, 21],
            [7, 2, 9, 11, 13, 15, 17, 21, 19],
            [11, 2, 4, 13, 21, 9, 17, 15, 19],
            [4, 6, 2, 11, 15, 19, 13, 17, 21],
            [6, 13, 15, 21, 19, 8, 4, 17, 2],
            [10, 8, 15, 17, 21, 6, 19, 2, 4],
            [17, 10, 12, 6, 19, 8, 21, 4, 2],
            [19, 14, 21, 10, 2, 4, 8, 6, 12],
            [21, 16, 4, 2, 12, 6, 14, 8, 10],
            [2, 23, 22, 16, 18, 14, 10, 4, 6, 8, 12],
            [20, 2, 16, 18, 14, 10, 12, 4, 8, 6],
        ],
    ),
    (
        [
            [-1, 2, 0, -1, -1, -1, -1, -1, -1, -1, -1, -1],
            [-1, -1, 1, -1, -1, -1, -1, -1, -1, -1, -1, -1],
            [-1, -1, -1, 2, 2, 3, 5, 10, 6, 10, 2, 10],
            [-1, -1, -1, -1, 3, 3, 9, 9, 9, 5, 9, 10],
            [-1, -1, -1, -1, -1, 4, 5, 5, 7, 6, 9, 9],
            [-1, -1, -1, -1, -1, -1, 5, 6, 9, 7, 9, 9],
            [-1, -1, -1, -1, -1, -1, -1, 6, 7, 7, 11, 9],
            [-1, -1, -1, -1, -1, -1, -1, -1, 9, 7, 9, 10],
            [-1, -1, -1, -1, -1, -1, -1, -1, -1, 8, 9, 10],
            [-1, -1, -1, -1, -1, -1, -1, -1, -1, -1, 11, 9],
            [-1, -1, -1, -1, -1, -1, -1, -1, -1, 10, -1, 10],
            [-1, -1, -1, -1, -1, -1, -1, -1, -1, 11, 11, -1],
        ],
        [
            [-1, -1, -1, -1, -1, -1, -1, -1, -1, -1, -1, -1],
            [1, -1, -1, -1, -1, -1, -1, -1, -1, -1, -1, -1],
            [2, 0, -1, -1, -1, -1, -1, -1, -1, -1, -1, -1],
            [1, 3, 1, -1, -1, -1, -1, -1, -1, -1, -1, -1],
            [2, 0, 4, 2, -1, -1, -1, -1, -1, -1, -1, -1],
            [4, 3, 3, 4, 5, -1, -1, -1, -1, -1, -1, -1],
            [2, 2, 6, 2, 2, 6, -1, -1, -1, -1, -1, -1],
            [1, 7, 3, 5, 5, 7, 5, -1, -1, -1, -1, -1],
            [1, 8, 1, 7, 5, 7, 7, 8, -1, -1, -1, -1],
            [9, 0, 0, 4, 9, 4, 5, 8, 9, -1, -1, -1],
            [-1, -1, -1, -1, -1, -1, -1, -1, -1, 10, -1, -1],
            [-1, -1, -1, -1, -1, -1, -1, -1, -1, 10, 11, -1],
        ],
        [
            [3, 5, 7, 9, 19, 11, 13, 15, 17],
            [7, 0, 15, 17, 5, 13, 9, 11, 19],
            [0, 2, 9, 7, 13, 17, 11, 15, 19],
            [4, 9, 11, 17, 13, 15, 19],
            [6, 11, 4, 19, 15, 13, 17],
            [6, 8, 13, 15, 4, 17, 19],
            [10, 8, 17, 15, 4, 19, 6],
            [12, 17, 10, 19, 8, 4, 6],
            [19, 12, 14, 8, 6, 4, 10],
            [21, 20, 14, 16, 12, 6, 22, 10, 4, 23, 8],
            [4, 23, 14, 22, 16, 18, 6, 10, 12, 8],
            [18, 20, 4, 12, 14, 16, 10, 6, 8],
        ],
    ),
    (
        [
            [-1, 0, 0, 2, -1, -1, -1, -1, -1, -1, -1, -1],
            [-1, -1, 1, 2, -1, -1, -1, -1, -1, -1, -1, -1],
            [-1, -1, -1, 2, -1, -1, -1, -1, -1, -1, -1, -1],
            [-1, -1, -1, -1, 5, 3, 5, 9, 9, 6, 9, 10],
            [-1, -1, -1, -1, -1, 6, 4, 8, 6, 8, 9, 7],
            [-1, -1, -1, -1, -1, -1, 5, 6, 7, 8, 11, 7],
            [-1, -1, -1, -1, -1, -1, -1, 8, 6, 8, 11, 9],
            [-1, -1, -1, -1, -1, -1, -1, -1, 9, 7, 11, 9],
            [-1, -1, -1, -1, -1, -1, -1, -1, -1, 8, 9, 10],
            [-1, -1, -1, -1, -1, -1, -1, -1, 10, -1, 9, 10],
            [-1, -1, -1, -1, -1, -1, -1, -1, 10, 11, -1, 10],
            [-1, -1, -1, -1, -1, -1, -1, -1, 10, 11, 11, -1],
        ],
        [
            [-1, -1, -1, -1, -1, -1, -1, -1, -1, -1, -1, -1],
            [1, -1, -1, -1, -1, -1, -1, -1, -1, -1, -1, -1],
            [2, 2, -1, -1, -1, -1, -1, -1, -1, -1, -1, -1],
            [3, 0, 0, -1, -1, -1, -1, -1, -1, -1, -1, -1],
            [2, 0, 4, 2, -1, -1, -1, -1, -1, -1, -1, -1],
            [2, 0, 5, 4, 2, -1, -1, -1, -1, -1, -1, -1],
            [2, 2, 6, 2, 2, 3, -1, -1, -1, -1, -1, -1],
            [7, 2, 7, 2, 5, 7, 7, -1, -1, -1, -1, -1],
            [8, 0, 5, 5, 5, 8, 5, 6, -1, -1, -1, -1],
            [-1, -1, -1, -1, -1, -1, -1, -1, 9, -1, -1, -1],
            [-1, -1, -1, -1, -1, -1, -1, -1, 10, 8, -1, -1],
            [-1, -1, -1, -1, -1, -1, -1, -1, 9, 10, 11, -1],
        ],
        [
            [3, 5, 7, 17, 9, 15, 11, 13],
            [0, 5, 7, 17, 13, 9, 15, 11],
            [0, 2, 9, 11, 13, 15, 7, 17],
            [4, 0, 2, 9, 13, 17, 15, 11],
            [6, 11, 17, 13, 15],
            [6, 17, 15, 8, 13],
            [8, 10, 6, 15, 17],
            [12, 10, 8, 17, 6],
            [19, 12, 21, 20, 8, 22, 14, 10, 23, 18, 6],
            [16, 22, 14, 23, 12, 21, 6, 8, 20, 10],
            [23, 22, 18, 16, 14, 6, 12, 8, 10],
            [20, 14, 18, 12, 16, 10, 8, 6],
        ],
    ),
    (
        [
            [-1, 0, 1, 1, 3, -1, -1, -1, -1, -1, -1, -1],
            [-1, -1, 1, 2, 2, -1, -1, -1, -1, -1, -1, -1],
            [-1, -1, -1, 2, 3, -1, -1, -1, -1, -1, -1, -1],
            [-1, -1, -1, -1, 3, -1, -1, -1, -1, -1, -1, -1],
            [-1, -1, -1, -1, -1, 6, 4, 8, 6, 10, 8, 10],
            [-1, -1, -1, -1, -1, -1, 5, 6, 6, 8, 7, 10],
            [-1, -1, -1, -1, -1, -1, -1, 6, 7, 10, 8, 10],
            [-1, -1, -1, -1, -1, -1, -1, -1, 9, 7, 9, 10],
            [-1, -1, -1, -1, -1, -1, -1, 8, -1, 11, 11, 8],
            [-1, -1, -1, -1, -1, -1, -1, 9, 9, -1, 11, 9],
            [-1, -1, -1, -1, -1, -1, -1, 9, 7, 10, -1, 10],
            [-1, -1, -1, -1, -1, -1, -1, 9, 9, 10, 11, -1],
        ],
        [
            [-1, -1, -1, -1, -1, -1, -1, -1, -1, -1, -1, -1],
            [1, -1, -1, -1, -1, -1, -1, -1, -1, -1, -1, -1],
            [2, 0, -1, -1, -1, -1, -1, -1, -1, -1, -1, -1],
            [3, 0, 3, -1, -1, -1, -1, -1, -1, -1, -1, -1],
            [4, 2, 4, 2, -1, -1, -1, -1, -1, -1, -1, -1],
            [4, 4, 4, 2, 5, -1, -1, -1, -1, -1, -1, -1],
            [1, 6, 1, 4, 5, 6, -1, -1, -1, -1, -1, -1],
            [7, 0, 4, 4, 7, 6, 7, -1, -1, -1, -1, -1],
            [-1, -1, -1, -1, -1, -1, -1, 8, -1, -1, -1, -1],
            [-1, -1, -1, -1, -1, -1, -1, 8, 9, -1, -1, -1],
            [-1, -1, -1, -1, -1, -1, -1, 8, 9, 10, -1, -1],
            [-1, -1, -1, -1, -1, -1, -1, 8, 9, 10, 11, -1],
        ],
        [
            [3, 5, 7, 9, 15, 11, 13],
            [0, 5, 7, 13, 11, 9, 15],
            [2, 0, 7, 9, 11, 13, 15],
            [0, 4, 2, 9, 15, 13, 11],
            [6, 11, 2, 15, 0, 4, 13],
            [13, 8, 15],
            [8, 10, 15],
            [12, 17, 16, 18, 19, 10, 20, 21, 8, 22, 23],
            [19, 18, 12, 21, 8, 14, 10, 23, 20, 22],
            [21, 20, 14, 23, 22, 16, 10, 12, 8],
            [23, 22, 14, 12, 8, 16, 10, 18],
            [16, 18, 20, 14, 12, 8, 10],
        ],
    ),
    (
        [
            [-1, 2, 0, 2, 2, 4, -1, -1, -1, -1, -1, -1],
            [-1, -1, 1, 2, 2, 3, -1, -1, -1, -1, -1, -1],
            [-1, -1, -1, 4, 2, 4, -1, -1, -1, -1, -1, -1],
            [-1, -1, -1, -1, 5, 3, -1, -1, -1, -1, -1, -1],
            [-1, -1, -1, -1, -1, 4, -1, -1, -1, -1, -1, -1],
            [-1, -1, -1, -1, -1, -1, 5, 8, 6, 7, 8, 10],
            [-1, -1, -1, -1, -1, -1, -1, 6, 7, 7, 8, 9],
            [-1, -1, -1, -1, -1, -1, 7, -1, 6, 8, 7, 10],
            [-1, -1, -1, -1, -1, -1, 7, 8, -1, 8, 8, 10],
            [-1, -1, -1, -1, -1, -1, 7, 9, 7, -1, 9, 10],
            [-1, -1, -1, -1, -1, -1, 7, 10, 7, 11, -1, 10],
            [-1, -1, -1, -1, -1, -1, 8, 8, 9, 11, 11, -1],
        ],
        [
            [-1, -1, -1, -1, -1, -1, -1, -1, -1, -1, -1, -1],
            [1, -1, -1, -1, -1, -1, -1, -1, -1, -1, -1, -1],
            [2, 0, -1, -1, -1, -1, -1, -1, -1, -1, -1, -1],
            [3, 0, 0, -1, -1, -1, -1, -1, -1, -1, -1, -1],
            [3, 3, 1, 4, -1, -1, -1, -1, -1, -1, -1, -1],
            [5, 0, 3, 5, 3, -1, -1, -1, -1, -1, -1, -1],
            [6, 4, 4, 4, 6, 6, -1, -1, -1, -1, -1, -1],
            [-1, -1, -1, -1, -1, -1, 7, -1, -1, -1, -1, -1],
            [-1, -1, -1, -1, -1, -1, 8, 6, -1, -1, -1, -1],
            [-1, -1, -1, -1, -1, -1, 7, 8, 9, -1, -1, -1],
            [-1, -1, -1, -1, -1, -1, 8, 8, 9, 10, -1, -1],
            [-1, -1, -1, -1, -1, -1, 7, 10, 10, 10, 11, -1],
        ],
        [
            [3, 5, 7, 11, 9, 13],
            [0, 5, 7, 9, 11, 13],
            [0, 2, 11, 7, 13, 9],
            [9, 0, 2, 11, 4, 13],
            [4, 0, 13, 2, 6, 11],
            [6, 8, 13, 4, 0, 2],
            [10, 15, 17, 14, 16, 18, 20, 21, 19, 23, 22],
            [12, 16, 18, 20, 19, 17, 23, 10, 21, 22],
            [19, 10, 21, 12, 23, 14, 22, 18, 20],
            [21, 22, 16, 12, 23, 20, 14, 10],
            [23, 22, 14, 16, 18, 10, 12],
            [20, 14, 16, 18, 12, 10],
        ],
    ),
    (
        [
            [-1, 0, 0, 1, 2, 4, 5, -1, -1, -1, -1, -1],
            [-1, -1, 1, 2, 3, 3, 4, -1, -1, -1, -1, -1],
            [-1, -1, -1, 2, 5, 3, 5, -1, -1, -1, -1, -1],
            [-1, -1, -1, -1, 5, 3, 5, -1, -1, -1, -1, -1],
            [-1, -1, -1, -1, -1, 4, 5, -1, -1, -1, -1, -1],
            [-1, -1, -1, -1, -1, -1, 5, -1, -1, -1, -1, -1],
            [-1, -1, -1, -1, -1, 6, -1, 6, 9, 6, 9, 9],
            [-1, -1, -1, -1, -1, 6, 7, -1, 7, 8, 9, 6],
            [-1, -1, -1, -1, -1, 7, 7, 9, -1, 8, 9, 9],
            [-1, -1, -1, -1, -1, 6, 10, 6, 10, -1, 9, 9],
            [-1, -1, -1, -1, -1, 7, 7, 8, 10, 11, -1, 10],
            [-1, -1, -1, -1, -1, 11, 5, 9, 9, 11, 11, -1],
        ],
        [
            [-1, -1, -1, -1, -1, -1, -1, -1, -1, -1, -1, -1],
            [1, -1, -1, -1, -1, -1, -1, -1, -1, -1, -1, -1],
            [1, 2, -1, -1, -1, -1, -1, -1, -1, -1, -1, -1],
            [3, 0, 3, -1, -1, -1, -1, -1, -1, -1, -1, -1],
            [4, 4, 1, 4, -1, -1, -1, -1, -1, -1, -1, -1],
            [4, 4, 4, 4, 5, -1, -1, -1, -1, -1, -1, -1],
            [-1, -1, -1, -1, -1, 6, -1, -1, -1, -1, -1, -1],
            [-1, -1, -1, -1, -1, 6, 7, -1, -1, -1, -1, -1],
            [-1, -1, -1, -1, -1, 6, 7, 8, -1, -1, -1, -1],
            [-1, -1, -1, -1, -1, 6, 9, 6, 7, -1, -1, -1],
            [-1, -1, -1, -1, -1, 6, 10, 6, 7, 6, -1, -1],
            [-1, -1, -1, -1, -1, 11, 5, 8, 10, 10, 11, -1],
        ],
        [
            [3, 7, 9, 5, 11],
            [0, 5, 9, 7, 11],
            [0, 2, 7, 11, 9],
            [4, 0, 2, 9, 11],
            [11, 0, 6, 4, 2],
            [6, 8, 13, 12, 4, 15, 14, 23, 19, 22, 21, 0, 17, 2, 16, 18, 20],
            [10, 15, 14, 19, 6, 21, 8, 17, 4, 18, 23, 16, 22, 2, 20, 0],
            [17, 12, 16, 19, 20, 21, 22, 18, 23],
            [14, 20, 18, 23, 22, 19, 12, 21],
            [16, 22, 12, 14, 23, 20, 21],
            [18, 23, 22, 16, 12, 14],
            [18, 20, 16, 14, 12],
        ],
    ),
    (
        [
            [-1, 0, 1, 2, 5, 2, 7, 5, -1, -1, -1, -1],
            [-1, -1, 3, 1, 3, 4, 5, 6, -1, -1, -1, -1],
            [-1, -1, -1, 4, 2, 4, 5, 6, -1, -1, -1, -1],
            [-1, -1, -1, -1, 3, 4, 5, 6, -1, -1, -1, -1],
            [-1, -1, -1, -1, -1, 4, 7, 5, -1, -1, -1, -1],
            [-1, -1, -1, -1, -1, -1, 5, 5, -1, -1, -1, -1],
            [-1, -1, -1, -1, -1, -1, -1, 6, -1, -1, -1, -1],
            [-1, -1, -1, -1, 6, 4, 7, -1, 9, 7, 9, 9],
            [-1, -1, -1, -1, 8, 4, 5, 8, -1, 7, 9, 7],
            [-1, -1, -1, -1, 10, 7, 7, 8, 9, -1, 9, 10],
            [-1, -1, -1, -1, 11, 6, 8, 9, 10, 11, -1, 10],
            [-1, -1, -1, -1, 11, 4, 8, 8, 11, 11, 11, -1],
        ],
        [
            [-1, -1, -1, -1, -1, -1, -1, -1, -1, -1, -1, -1],
            [1, -1, -1, -1, -1, -1, -1, -1, -1, -1, -1, -1],
            [1, 2, -1, -1, -1, -1, -1, -1, -1, -1, -1, -1],
            [2, 2, 3, -1, -1, -1, -1, -1, -1, -1, -1, -1],
            [4, 3, 3, 4, -1, -1, -1, -1, -1, -1, -1, -1],
            [-1, -1, -1, -1, 5, -1, -1, -1, -1, -1, -1, -1],
            [-1, -1, -1, -1, 6, 6, -1, -1, -1, -1, -1, -1],
            [-1, -1, -1, -1, 6, 4, 7, -1, -1, -1, -1, -1],
            [-1, -1, -1, -1, 6, 6, 8, 6, -1, -1, -1, -1],
            [-1, -1, -1, -1, 6, 6, 8, 6, 9, -1, -1, -1],
            [-1, -1, -1, -1, 10, 4, 5, 8, 9, 10, -1, -1],
            [-1, -1, -1, -1, 11, 4, 5, 8, 10, 10, 11, -1],
        ],
        [
            [3, 9, 7, 5],
            [0, 5, 7, 9],
            [0, 7, 2, 9],
            [2, 9, 0, 4],
            [6, 4, 11, 2, 13, 16, 21, 17, 23, 0, 22, 15, 18, 14, 20, 19],
            [8, 13, 0, 6, 4, 2, 17, 16, 21, 23, 19, 22, 18, 15, 20, 14],
            [10, 17, 15, 14, 19, 6, 20, 4, 8, 2, 22, 16, 18, 21, 0, 23],
            [10, 16, 12, 8, 17, 18, 0, 19, 22, 21, 6, 23, 4, 20, 2],
            [19, 18, 20, 22, 21, 23, 14],
            [21, 14, 22, 23, 16, 20],
            [18, 23, 22, 14, 16],
            [20, 18, 14, 16],
        ],
    ),
    (
        [
            [-1, 2, 0, 2, 3, 2, 5, 6, 6, -1, -1, -1],
            [-1, -1, 3, 1, 3, 3, 5, 6, 6, -1, -1, -1],
            [-1, -1, -1, 4, 5, 2, 7, 5, 7, -1, -1, -1],
            [-1, -1, -1, -1, 5, 3, 5, 8, 6, -1, -1, -1],
            [-1, -1, -1, -1, -1, 4, 5, 8, 6, -1, -1, -1],
            [-1, -1, -1, -1, -1, -1, 5, 6, 7, -1, -1, -1],
            [-1, -1, -1, -1, -1, -1, -1, 6, 6, -1, -1, -1],
            [-1, -1, -1, -1, -1, -1, -1, -1, 7, -1, -1, -1],
            [-1, -1, -1, 9, 3, 6, 7, 9, -1, 8, 9, 10],
            [-1, -1, -1, 10, 5, 7, 5, 9, 7, -1, 9, 9],
            [-1, -1, -1, 9, 5, 7, 5, 10, 9, 10, -1, 10],
            [-1, -1, -1, 4, 11, 4, 7, 9, 9, 11, 11, -1],
        ],
        [
            [-1, -1, -1, -1, -1, -1, -1, -1, -1, -1, -1, -1],
            [1, -1, -1, -1, -1, -1, -1, -1, -1, -1, -1, -1],
            [1, 2, -1, -1, -1, -1, -1, -1, -1, -1, -1, -1],
            [1, 3, 3, -1, -1, -1, -1, -1, -1, -1, -1, -1],
            [-1, -1, -1, 4, -1, -1, -1, -1, -1, -1, -1, -1],
            [-1, -1, -1, 4, 5, -1, -1, -1, -1, -1, -1, -1],
            [-1, -1, -1, 4, 6, 6, -1, -1, -1, -1, -1, -1],
            [-1, -1, -1, 5, 3, 7, 7, -1, -1, -1, -1, -1],
            [-1, -1, -1, 5, 5, 7, 5, 8, -1, -1, -1, -1],
            [-1, -1, -1, 5, 5, 7, 5, 9, 7, -1, -1, -1],
            [-1, -1, -1, 9, 3, 7, 7, 9, 7, 10, -1, -1],
            [-1, -1, -1, 11, 3, 3, 5, 9, 9, 10, 11, -1],
        ],
        [
            [3, 5, 7],
            [5, 7, 0],
            [0, 7, 2],
            [2, 9, 0, 11, 23, 13, 15, 4, 16, 18, 17, 22, 21, 19, 20],
            [11, 13, 2, 4, 6, 22, 0, 23, 17, 15, 19, 16, 18, 20, 21],
            [4, 13, 6, 15, 8, 0, 17, 2, 19, 18, 20, 23, 22, 21, 16],
            [10, 15, 6, 8, 0, 17, 4, 2, 16, 19, 18, 21, 20, 22, 23],
            [12, 17, 19, 18, 10, 20, 4, 16, 21, 22, 0, 23, 6, 2, 8],
            [12, 14, 19, 18, 20, 10, 4, 22, 6, 8, 23, 21, 0, 2],
            [16, 21, 20, 22, 23],
            [18, 23, 22, 16],
            [18, 20, 16],
        ],
    ),
    (
        [
            [-1, 2, 0, 2, 3, 4, 5, 8, 3, 8, -1, -1],
            [-1, -1, 3, 1, 5, 6, 3, 8, 6, 8, -1, -1],
            [-1, -1, -1, 2, 3, 4, 7, 5, 7, 7, -1, -1],
            [-1, -1, -1, -1, 3, 4, 7, 5, 7, 8, -1, -1],
            [-1, -1, -1, -1, -1, 4, 7, 5, 7, 7, -1, -1],
            [-1, -1, -1, -1, -1, -1, 5, 5, 9, 7, -1, -1],
            [-1, -1, -1, -1, -1, -1, -1, 8, 6, 8, -1, -1],
            [-1, -1, -1, -1, -1, -1, -1, -1, 9, 7, -1, -1],
            [-1, -1, -1, -1, -1, -1, -1, -1, -1, 8, -1, -1],
            [-1, -1, 10, 2, 5, 6, 9, 5, 10, -1, 9, 10],
            [-1, -1, 10, 4, 2, 4, 8, 6, 10, 8, -1, 10],
            [-1, -1, 10, 11, 3, 6, 10, 8, 10, 8, 11, -1],
        ],
        [
            [-1, -1, -1, -1, -1, -1, -1, -1, -1, -1, -1, -1],
            [1, -1, -1, -1, -1, -1, -1, -1, -1, -1, -1, -1],
            [2, 2, -1, -1, -1, -1, -1, -1, -1, -1, -1, -1],
            [-1, -1, 3, -1, -1, -1, -1, -1, -1, -1, -1, -1],
            [-1, -1, 4, 4, -1, -1, -1, -1, -1, -1, -1, -1],
            [-1, -1, 3, 5, 5, -1, -1, -1, -1, -1, -1, -1],
            [-1, -1, 4, 2, 6, 6, -1, -1, -1, -1, -1, -1],
            [-1, -1, 3, 6, 3, 4, 7, -1, -1, -1, -1, -1],
            [-1, -1, 4, 4, 6, 4, 8, 5, -1, -1, -1, -1],
            [-1, -1, 3, 6, 5, 6, 9, 6, 7, -1, -1, -1],
            [-1, -1, 9, 2, 2, 6, 8, 8, 9, 10, -1, -1],
            [-1, -1, 11, 2, 3, 3, 7, 8, 11, 10, 11, -1],
        ],
        [
            [3, 5],
            [5, 0],
            [0, 9, 7, 2, 20, 11, 23, 18, 13, 21, 15, 17, 22, 19],
            [2, 4, 0, 9, 11, 15, 22, 19, 23, 18, 17, 13, 20, 21],
            [6, 11, 4, 13, 0, 17, 20, 15, 22, 19, 2, 23, 18, 21],
            [8, 13, 6, 4, 19, 0, 2, 18, 17, 20, 23, 22, 15, 21],
            [10, 15, 17, 19, 2, 18, 20, 8, 22, 0, 21, 23, 6, 4],
            [10, 8, 19, 12, 23, 6, 4, 21, 20, 0, 18, 2, 17, 22],
            [20, 12, 23, 18, 21, 0, 2, 22, 8, 14, 19, 10, 6, 4],
            [21, 14, 16, 23, 10, 20, 12, 8, 0, 2, 22, 4, 6],
            [18, 23, 22],
            [20, 18],
        ],
    ),
    (
        [
            [-1, 2, 0, 0, 3, 4, 2, 6, 9, 1, 9, -1],
            [-1, -1, 1, 2, 3, 2, 5, 6, 10, 10, 2, -1],
            [-1, -1, -1, 4, 5, 2, 5, 8, 6, 8, 8, -1],
            [-1, -1, -1, -1, 3, 7, 4, 6, 7, 6, 9, -1],
            [-1, -1, -1, -1, -1, 7, 5, 4, 7, 8, 9, -1],
            [-1, -1, -1, -1, -1, -1, 7, 5, 6, 7, 9, -1],
            [-1, -1, -1, -1, -1, -1, -1, 6, 7, 7, 9, -1],
            [-1, -1, -1, -1, -1, -1, -1, -1, 7, 7, 9, -1],
            [-1, -1, -1, -1, -1, -1, -1, -1, -1, 8, 9, -1],
            [-1, -1, -1, -1, -1, -1, -1, -1, -1, -1, 9, -1],
            [-1, 10, 1, 2, 5, 7, 5, 10, 10, 10, -1, 1],
            [-1, 9, 11, 2, 5, 9, 9, 6, 9, 11, 11, -1],
        ],
        [
            [-1, -1, -1, -1, -1, -1, -1, -1, -1, -1, -1, -1],
            [1, -1, -1, -1, -1, -1, -1, -1, -1, -1, -1, -1],
            [-1, 2, -1, -1, -1, -1, -1, -1, -1, -1, -1, -1],
            [-1, 2, 3, -1, -1, -1, -1, -1, -1, -1, -1, -1],
            [-1, 2, 3, 4, -1, -1, -1, -1, -1, -1, -1, -1],
            [-1, 3, 1, 5, 3, -1, -1, -1, -1, -1, -1, -1],
            [-1, 3, 3, 6, 3, 6, -1, -1, -1, -1, -1, -1],
            [-1, 4, 4, 5, 6, 6, 7, -1, -1, -1, -1, -1],
            [-1, 2, 4, 2, 8, 4, 5, 8, -1, -1, -1, -1],
            [-1, 8, 1, 7, 5, 7, 5, 8, 9, -1, -1, -1],
            [-1, 2, 10, 2, 2, 3, 4, 8, 10, 8, -1, -1],
            [-1, 11, 11, 2, 3, 3, 7, 8, 10, 8, 11, -1],
        ],
        [
            [3],
            [5, 0, 7, 20, 23, 11, 13, 9, 19, 21, 15, 17, 22],
            [0, 7, 2, 9, 21, 13, 23, 17, 22, 20, 11, 15, 19],
            [0, 9, 11, 13, 2, 21, 23, 19, 17, 15, 22, 4, 20],
            [6, 17, 0, 15, 4, 11, 13, 21, 2, 20, 23, 19, 22],
            [13, 4, 15, 8, 2, 17, 20, 0, 19, 22, 21, 6, 23],
            [15, 0, 6, 4, 10, 8, 2, 17, 22, 20, 21, 19, 23],
            [8, 17, 10, 12, 20, 19, 21, 0, 6, 23, 2, 4, 22],
            [14, 19, 21, 20, 8, 23, 12, 22, 4, 2, 10, 0, 6],
            [14, 16, 20, 22, 21, 10, 0, 12, 8, 6, 23, 2, 4],
            [18, 23, 22, 14, 2, 16, 10, 0, 12, 8, 6, 4],
            [20],
        ],
    ),
    (
        [
            [-1, 0, 4, 4, 0, 4, 4, 6, 10, 11, 11, 1],
            [-1, -1, 1, 4, 1, 4, 4, 9, 9, 11, 7, 1],
            [-1, -1, -1, 4, 2, 4, 5, 8, 6, 8, 8, 10],
            [-1, -1, -1, -1, 3, 4, 5, 6, 7, 8, 6, 10],
            [-1, -1, -1, -1, -1, 6, 4, 6, 4, 11, 11, 8],
            [-1, -1, -1, -1, -1, -1, 5, 6, 6, 10, 8, 10],
            [-1, -1, -1, -1, -1, -1, -1, 6, 7, 7, 9, 10],
            [-1, -1, -1, -1, -1, -1, -1, -1, 7, 10, 8, 10],
            [-1, -1, -1, -1, -1, -1, -1, -1, -1, 8, 9, 10],
            [-1, -1, -1, -1, -1, -1, -1, -1, -1, -1, 9, 10],
            [-1, -1, -1, -1, -1, -1, -1, -1, -1, -1, -1, 10],
            [11, 0, 0, 4, 9, 7, 7, 9, 9, 11, 9, -1],
        ],
        [
            [-1, -1, -1, -1, -1, -1, -1, -1, -1, -1, -1, -1],
            [1, -1, -1, -1, -1, -1, -1, -1, -1, -1, -1, -1],
            [2, 2, -1, -1, -1, -1, -1, -1, -1, -1, -1, -1],
            [1, 3, 3, -1, -1, -1, -1, -1, -1, -1, -1, -1],
            [2, 0, 4, 2, -1, -1, -1, -1, -1, -1, -1, -1],
            [1, 2, 5, 4, 5, -1, -1, -1, -1, -1, -1, -1],
            [1, 2, 6, 2, 3, 3, -1, -1, -1, -1, -1, -1],
            [1, 3, 3, 7, 5, 7, 5, -1, -1, -1, -1, -1],
            [2, 2, 8, 2, 5, 7, 5, 8, -1, -1, -1, -1],
            [8, 3, 3, 9, 3, 7, 5, 8, 9, -1, -1, -1],
            [10, 0, 4, 4, 7, 4, 7, 10, 10, 8, -1, -1],
            [11, 11, 1, 1, 6, 6, 8, 6, 9, 11, 0, -1],
        ],
        [
            [5, 3, 7, 21, 23, 9, 11, 22, 19, 17, 13, 15],
            [5, 7, 0, 11, 13, 15, 23, 21, 17, 9, 19, 22],
            [7, 11, 9, 13, 17, 2, 15, 0, 19, 23, 21, 22],
            [15, 4, 11, 19, 0, 9, 13, 17, 21, 2, 23, 22],
            [4, 6, 11, 0, 21, 15, 2, 19, 22, 17, 13, 23],
            [4, 15, 6, 17, 8, 0, 19, 21, 2, 22, 13, 23],
            [10, 8, 4, 15, 21, 6, 0, 17, 23, 19, 22, 2],
            [17, 21, 12, 19, 10, 8, 22, 6, 2, 0, 4, 23],
            [19, 21, 8, 14, 10, 23, 12, 22, 4, 2, 0, 6],
            [16, 23, 22, 2, 21, 0, 12, 4, 8, 14, 10, 6],
            [18, 16, 0, 23, 22, 14, 10, 6, 8, 12, 4, 2],
            [2, 0, 20, 8, 18, 16, 14, 10, 6, 12, 4],
        ],
    ),
]


def word(plan, chip, code):
    source = plan[code % 2][code // 2]
    to = [w for w in range(len(source)) if source[w] == chip]
    to = sorted(to, key=lambda w: (w > chip) * 100 + w)
    to = to + [NONE] * (4 - len(to))
    return code + 32 * (to[0] + 16 * (to[1] + 16 * (to[2] + 16 * to[3])))


def kernel(
    plan, chips,
    doc_ref, q_hbm, k_hbm, v_hbm, out_ref,
    q_ref, kv, acc, peak, total, give, give_at, take, take_at,
    load_sem, ring_send, ring_recv, mate_send, mate_recv, q_sem, side_send, side_recv,
):
    ctx, tp = lax.axis_index("ctx"), lax.axis_index("tp")
    z, core = ctx // 2, ctx % 2
    other = 1 - core
    odd = tp % 2
    shards = 2 * chips
    mate = (2 * z + other, tp)
    side = (ctx, tp + 1 - 2 * odd)
    order = plan[2]

    loads = []
    for kind in (1, 0):
        for part, hbm in enumerate((k_hbm, v_hbm)):
            half = hbm.at[pl.ds(pl.multiple_of(kind * SPAN + odd * BLK, BLK), BLK)]
            loads.append(
                pltpu.make_async_copy(half, kv.at[z, kind, part, core], load_sem.at[2 * kind + part])
            )
    loads.append(pltpu.make_async_copy(q_hbm, q_ref.at[:, 0], load_sem.at[4]))
    for copy in loads:
        copy.start()

    def by_chip(values):
        return functools.reduce(lambda a, i: jnp.where(z == i, values[i], a), range(1, chips), jnp.int32(values[0]))

    def chip(w):
        return (2 * w + core, tp)

    parents = [sorted({t[s][w] for t in plan[:2] for s in range(chips)} - {-1}) for w in range(chips)]
    targets = [sum(w in p for p in parents) for w in range(chips)]

    barrier = pltpu.get_barrier_semaphore()
    for neighbour in (mate, side):
        pl.semaphore_signal(barrier, inc=1, device_id=neighbour, device_id_type=MESH)

    def greet(w, left):
        @pl.when(lax.rem(left, 2) == 1)
        def _():
            pl.semaphore_signal(barrier, inc=1, device_id=chip(w), device_id_type=MESH)

        return lax.div(left, 2)

    lax.fori_loop(0, chips, greet, by_chip([sum(1 << p for p in ps) for ps in parents]))

    steps = max(map(len, order))
    words = [by_chip([word(plan, w, o[e]) if e < len(o) else 0 for w, o in enumerate(order)]) for e in range(steps)]
    own_words = [by_chip([word(plan, w, 2 * w + kind) for w in range(chips)]) for kind in range(2)]
    count = by_chip([len(o) for o in order])
    pl.semaphore_wait(barrier, by_chip(targets) + 2)

    def remote(src, dst, send_sem, recv_sem, device):
        return pltpu.make_async_remote_copy(
            src_ref=src, dst_ref=dst, send_sem=send_sem, recv_sem=recv_sem, device_id=device, device_id_type=MESH
        )

    def ring_copy(s, kind, j, device):
        piece = kv.at[s, kind, :, core]
        return remote(piece, piece, ring_send.at[s, kind, j], ring_recv.at[s, kind], device)

    def mate_copy(s, kind, who):
        piece = kv.at[s, kind, :, who]
        return remote(piece, piece, mate_send.at[s, kind], mate_recv.at[s, kind], mate)

    def side_copies(n):
        return [
            remote(give.at[n], take.at[n], side_send.at[n, 0], side_recv.at[n, 0], side),
            remote(give_at.at[n], take_at.at[n], side_send.at[n, 1], side_recv.at[n, 1], side),
        ]

    def each_child(w, act):
        code = lax.rem(w, 32)
        for j in range(4):
            to = lax.rem(lax.div(w, 32 * 16**j), 16)

            @pl.when(to < NONE)
            def _():
                act(ring_copy(lax.div(code, 2), lax.rem(code, 2), j, chip(to)))

    for kind in (1, 0):
        for copy in loads[2 * (1 - kind) : 2 * (1 - kind) + 2]:
            copy.wait()
        each_child(own_words[kind], lambda copy: copy.start())
        mate_copy(z, kind, core).start()
    loads[4].wait()
    q_copy = remote(q_ref.at[:, 0], q_ref.at[:, 1], q_sem.at[0], q_sem.at[1], side)
    q_copy.start()

    def key_block(s, kind, j):
        span = 2 * s + j
        return jnp.where(kind == 0, 2 * span, 2 * (2 * shards - 1 - span)) + odd

    def query_block(n):
        return jnp.where(n < 2, 2 * ctx, 2 * (2 * shards - 1 - ctx) - 2) + n

    def scored(n, s_chip, kind):
        k = kv[s_chip, kind, 0].reshape(2 * BLK, HD)
        q = q_ref[n].reshape(2 * BLK, HD)
        s = lax.dot_general(q, k, (((1,), (1,)), ((), ())), preferred_element_type=jnp.float32)
        return [s[:, j * BLK : (j + 1) * BLK] * SCALE for j in range(2)]

    def summed(weights, s_chip, kind):
        joined = jnp.concatenate([w.astype(jnp.bfloat16) for w in weights], axis=1)
        v = kv[s_chip, kind, 1].reshape(2 * BLK, HD)
        return jnp.dot(joined, v, preferred_element_type=jnp.float32)

    def own(n, kind):
        parts = scored(n, z, kind)
        q_block = query_block(n)
        row = lax.broadcasted_iota(jnp.int32, (2, BLK, BLK), 1).reshape(2 * BLK, BLK)
        inside = lax.broadcasted_iota(jnp.int32, (2 * BLK, BLK), 1) <= row
        for j in range(2):
            k_block = key_block(z, kind, j)
            same = doc_ref[k_block] == doc_ref[q_block]
            before = jnp.where(same & (k_block < q_block), 0.0, NEG)
            at_or_before = jnp.where(same & (k_block <= q_block), 0.0, NEG)
            parts[j] = parts[j] + jnp.where(inside, at_or_before, before)
        most = jnp.max(functools.reduce(jnp.maximum, parts), axis=1, keepdims=True)
        top = jnp.broadcast_to(jnp.maximum(most, FLOOR), (2 * BLK, HD))
        weights = [jnp.exp2(part - top) for part in parts]
        peak[n] = top
        total[n] = functools.reduce(jnp.add, weights)
        acc[n] = summed(weights, z, kind)

    def unit(n, s_chip, kind):
        parts = scored(n, s_chip, kind)
        q_block = query_block(n)
        for j in range(2):
            same = doc_ref[key_block(s_chip, kind, j)] == doc_ref[q_block]
            parts[j] = parts[j] + jnp.where(same, 0.0, NEG)
        old = peak[n]
        top = jnp.maximum(old, jnp.max(functools.reduce(jnp.maximum, parts), axis=1, keepdims=True))
        shrink = jnp.exp2(old - top)
        weights = [jnp.exp2(part - top) for part in parts]
        peak[n] = top
        total[n] = total[n] * shrink + functools.reduce(jnp.add, weights)
        acc[n] = acc[n] * shrink + summed(weights, s_chip, kind)

    def units(s, kind):
        low = (kind == 0) & (s < z)
        high = (kind == 1) | (s + z >= chips - 1)

        def pair(m, carry):
            for half in range(2):
                unit(2 * m + half, s, kind)
            return carry

        lax.fori_loop(jnp.where(low, 0, 1), jnp.where(high, 2, 1), pair, 0)

    def pick(e):
        w = functools.reduce(lambda a, i: jnp.where(e == i, words[i], a), range(1, steps), words[0])
        code = lax.rem(w, 32)
        return w, lax.div(code, 2), lax.rem(code, 2)

    def step(e, carry):
        @pl.when(e < count)
        def _():
            w, s, kind = pick(e)
            ring_copy(s, kind, 0, mate).wait_recv()
            each_child(w, lambda copy: copy.start())
            mate_copy(s, kind, core).start()

        @pl.when(e == 0)
        def _():
            q_copy.wait_recv()
            for kind in range(2):
                mate_copy(z, kind, other).wait_recv()

            def pair(m, carry):
                for half in range(2):
                    own(2 * m + half, m)
                return carry

            lax.fori_loop(0, 2, pair, 0)

            @pl.when(z + z >= chips - 1)
            def _():
                units(z, 0)

        @pl.when(e >= 1)
        def _():
            _, s, kind = pick(e - 1)
            mate_copy(s, kind, other).wait_recv()
            units(s, kind)

        return carry

    lax.fori_loop(0, count + 1, step, 0)

    def part(n, head):
        rows = pl.ds(head * BLK, BLK)
        mass = jnp.maximum(jnp.sum(total[n, rows], axis=1, keepdims=True), 1e-30)
        return acc[n, rows] / mass, peak[n, rows] + jnp.log(mass) * LOG2E

    for n in range(4):
        mixed, level = part(n, 1)
        give[n] = mixed.astype(jnp.bfloat16)
        give_at[n] = jnp.transpose(level)[:8]
        if n:
            for copy in side_copies(n - 1):
                copy.start()
    for copy in side_copies(3):
        copy.start()

    for n in range(4):
        mixed, level = part(n, 0)
        for copy in side_copies(n):
            copy.wait_recv()
        their_level = jnp.transpose(jnp.broadcast_to(take_at[n, 0:1], (BLK, HD)))
        top = jnp.maximum(level, their_level)
        ours, theirs = jnp.exp2(level - top), jnp.exp2(their_level - top)
        result = (mixed * ours + take[n].astype(jnp.float32) * theirs) / (ours + theirs)
        out_ref[n * BLK : (n + 1) * BLK] = result.astype(out_ref.dtype)

    q_copy.wait_send()
    for kind in range(2):
        each_child(own_words[kind], lambda copy: copy.wait_send())
        mate_copy(z, kind, core).wait_send()
    for n in range(4):
        for copy in side_copies(n):
            copy.wait_send()

    def drain(e, carry):
        w, s, kind = pick(e)
        each_child(w, lambda copy: copy.wait_send())
        mate_copy(s, kind, core).wait_send()
        return carry

    lax.fori_loop(0, count, drain, 0)


def call(ident, queries, keys, values, doc_blocks):
    rows = queries.shape[0]
    blocks = rows // BLK
    chips = lax.axis_size("ctx") // 2
    dma = pltpu.SemaphoreType.DMA
    return pl.pallas_call(
        functools.partial(kernel, PLANS[ident], chips),
        out_shape=pltpu.VMEM((rows, HD), jnp.bfloat16),
        in_specs=[pl.BlockSpec(memory_space=pltpu.SMEM)] + [pl.BlockSpec(memory_space=pl.ANY)] * 3,
        out_specs=pl.BlockSpec(memory_space=pltpu.VMEM),
        scratch_shapes=[
            pltpu.VMEM((blocks, 2, BLK, HD), jnp.bfloat16),
            pltpu.VMEM((chips, 2, 2, 2, BLK, HD), jnp.bfloat16),
            pltpu.VMEM((blocks, 2 * BLK, HD), jnp.float32),
            pltpu.VMEM((blocks, 2 * BLK, HD), jnp.float32),
            pltpu.VMEM((blocks, 2 * BLK, HD), jnp.float32),
            pltpu.VMEM((blocks, BLK, HD), jnp.bfloat16),
            pltpu.VMEM((blocks, 8, BLK), jnp.float32),
            pltpu.VMEM((blocks, BLK, HD), jnp.bfloat16),
            pltpu.VMEM((blocks, 8, BLK), jnp.float32),
            dma((5,)),
            dma((chips, 2, 4)),
            dma((chips, 2)),
            dma((chips, 2)),
            dma((chips, 2)),
            dma((2,)),
            dma((blocks, 2)),
            dma((blocks, 2)),
        ],
        compiler_params=pltpu.CompilerParams(collective_id=ident, has_side_effects=True),
    )(doc_blocks, queries.reshape(blocks, BLK, HD), keys, values)


def body(queries, keys, values, doc_blocks):
    starts = doc_blocks.shape[0] - LONGEST + 1
    whole = doc_blocks[:starts] == doc_blocks[LONGEST - 1 :]
    plans = lax.rem(lax.div(lax.iota(jnp.int32, starts), jnp.int32(STARTS)), jnp.int32(len(PLANS)))
    which = jnp.max(jnp.where(whole, plans, 0))
    return lax.switch(
        which, [functools.partial(call, i) for i in range(len(PLANS))], queries, keys, values, doc_blocks
    )


def solution(mesh):
    return jax.shard_map(
        body,
        mesh=mesh,
        in_specs=(P("ctx", "tp"), P("ctx", "tp"), P("ctx", "tp"), P()),
        out_specs=P("ctx", "tp"),
        check_vma=False,
    )
```

time: 181 us -> 45.8 us (0.25)
  the two profiles are of different devices: /device:TPU:1 before, /device:TPU:151 now
where the time goes in v2:
time: 45.8 us; the launch traced here: 45.6 us
  Pallas kernels  42.3 us (92%)
  other arithmetic  1.44 us (3%)
  between operations  0.69 us (2%)
  local copies, waits for them, and re-layouts  0.66 us (1%)
  loops' own time  0.58 us (1%)
    pallas_call x1, Pallas kernels, call(): pl.pallas_call(functools.partial(kernel, PLANS[ident], chips), out_shape=...  42.3 us
    reduce_max x1, other arithmetic, body(): which = jnp.max(jnp.where(whole, plans, 0))  1.44 us

profile of v2, /device:TPU:151, one launch (start us, length us, event | category | flops | bytes accessed | tf_op | source)
XLA Modules:
  0.0 45.6 jit_solution(17209966233716687469)
XLA Ops:
  0.0 1.4 %fusion = s32[]{:T(128)} fusion(s32[96]{0:T(128)} %param.19), kind=kLoop, calls=%fused_computation.1 | loop fusion | flops 244 | bytes 396 | tf_op jit(solution)/shard_map/reduce_max | solution.py:833
  1.4 0.0 copy-start
  2.1 0.0 copy-done
  2.1 42.8 %conditional.1 = (bf16[512,128]{1,0:T(8,128)(2,1)S(1)}) conditional(s32[]{:T(128)} %clamp.3, (bf16[512,128]{1,0:T(8,128)(2,1)}, s32[96]{0:T(128)S(1)}, bf16[512,128]{1,0:T(8,128)(2,1)}, bf16[512,128]{1,0:T(8,128)(2,1)}) %tuple.66, (bf16[512,128]{1,0:T(8,128)(2,1)}, s32[96]{0:T(128)S(1)}, bf16[512,128]{1,0:T(8,128)(2,1)}, ...), branch_computations={%region_1.2_spmd, %region_2.3_spmd, %region_3.4_spmd, %region_4.5_... | conditional | bytes 8 | solution.py:834
  2.2 42.3 %branch_2_fun.1 = bf16[512,128]{1,0:T(8,128)(2,1)S(1)} custom-call(s32[96]{0:T(128)S(1)} %get-tuple-element.120.doc_ref, bf16[4,128,128]{2,1,0:T(8,128)(2,1)} %bitcast.14, bf16[512,128]{1,0:T(8,128)(2,1)} %get-tuple-element.124.k_hbm, bf16[512,128]{1,0:T(8,128)(2,1)} %get-tuple-element.125.v_hbm), custom_call_target="tpu_custom_call" | custom-call | tf_op jit(solution)/shard_map/cond/branch_2_fun/pallas_call | solution.py:801
  45.0 0.7 %copy.30 = bf16[512,128]{1,0:T(8,128)(2,1)} copy(bf16[512,128]{1,0:T(8,128)(2,1)S(1)} %get-tuple-element.162) | data formatting | bytes 262144
Async XLA Ops:
  1.4 0.7 %copy-start = (s32[96]{0:T(128)S(1)}, s32[96]{0:T(128)}, u32[]{:S(2)}) copy-start(s32[96]{0:T(128)} %param.19) | copy-start | bytes 1156
